TPU v7x, 128 devices: a whole 4x4x4 slice. The times are simulated.
128 devices in a mesh: shard: 32 (over y, z, core), rep: 4 (over x).
Axes of the slice: x: 4, y: 4, z: 4, core: 2. Of those that a mesh axis runs over, the one named last changes fastest.
Arguments:
- feats: bfloat16 [32768, 768], P('shard'), may hold values from -6 to 6
- bases: bfloat16 [4, 768, 1024], P(None, None, 'rep'), may hold values from -0.21875 to 0.21875
- coef: bfloat16 [5, 4], replicated, may hold values from -2 to 2
- root_weight: bfloat16 [768, 1024], P(None, 'rep'), may hold values from -0.21875 to 0.21875
- slot_block: int32 [32, 32, 2], P('shard'), may hold values from 0 to 7
- recv_rel: int32 [32, 32, 2], P('shard'), may hold values from 0 to 4
- tile_slot: int32 [32, 256], P('shard'), may hold values from 0 to 63, as said below
- tile_dst: int32 [32, 256], P('shard'), may hold values from 0 to 7
- tile_adj: bfloat16 [32, 256, 128, 128], P('shard'), may hold values from 0 to 0.049804688
- d_out: bfloat16 [32768, 1024], P('shard', 'rep'), may hold values from -6 to 6
Outputs:
- output: bfloat16 [32768, 1024], P('shard', 'rep')
- grad_feats: bfloat16 [32768, 768], P(('shard', 'rep'))
- grad_bases: float32 [4, 768, 1024], P(None, 'shard', 'rep')
- grad_root: float32 [768, 1024], P('shard', 'rep')
- grad_coef: float32 [5, 4], replicated
Inputs may be any that keep to these rules, and one draw needn't show every extreme that they name: `tile_slot`: in each row (one destination device) every one of the 64 slots is named by at least one tile.
All inputs are finite; a program needn't handle non-finite values.
Results may differ from a plain program's by a relative error of at most 0.0062.
Values may be sent and summed in bfloat16 or wider, within the bound.
No kernel may reach another device: no remote copies, remote signals or barrier semaphores. Data moves between devices by JAX's collectives and lax.ppermute only.
A program may use at most 192 MiB of HBM per device.

v0:
```python
import jax
import jax.numpy as jnp
from jax import lax
from jax.sharding import PartitionSpec as P

BLK = 128
highest = lax.Precision.HIGHEST


def project_slots(source, weights):
    return jnp.einsum("snc,sco->sno", source, weights, preferred_element_type=jnp.float32).astype(
        jnp.bfloat16
    )


def body(
    feats, bases, coef, root_weight, slot_block, recv_rel, tile_slot, tile_dst, tile_adj, d_out
):
    shards = lax.axis_size("shard")
    nblocks = feats.shape[0] // BLK
    width_in = feats.shape[1]
    width_out = root_weight.shape[1]
    relations = coef.shape[0]
    capacity = slot_block.shape[2]
    slot_count = shards * capacity
    rel_weights = (
        jnp.dot(coef, bases.reshape(bases.shape[0], -1), preferred_element_type=jnp.float32)
        .astype(jnp.bfloat16)
        .reshape(relations, width_in, width_out)
    )
    feat_blocks = feats.reshape(nblocks, BLK, width_in)
    send_block = slot_block[0]
    local_rel = recv_rel[0]
    owner_rel = lax.all_to_all(local_rel, "shard", split_axis=0, concat_axis=0, tiled=True)
    tile_ids = tile_slot[0]
    dest_ids = tile_dst[0]
    adjacency = tile_adj[0]
    root_term = jnp.dot(feats, root_weight, preferred_element_type=jnp.float32)
    slot_weights = rel_weights[local_rel.reshape(-1)]
    outgoing = feat_blocks[send_block]
    incoming = lax.all_to_all(outgoing, "shard", split_axis=0, concat_axis=0, tiled=True)
    slot_msgs = project_slots(incoming.reshape(slot_count, BLK, width_in), slot_weights)
    tile_msgs = slot_msgs[tile_ids]
    weighted = jnp.einsum("tij,tjo->tio", adjacency, tile_msgs, preferred_element_type=jnp.float32)
    dst_onehot = (dest_ids[:, None] == jnp.arange(nblocks)[None, :]).astype(jnp.float32)
    neighbor_sum = jnp.einsum("tb,tio->bio", dst_onehot, weighted, precision=highest).reshape(
        -1, width_out
    )
    output = (neighbor_sum + root_term).astype(jnp.bfloat16)
    grad_rows = d_out.reshape(nblocks, BLK, width_out)[dest_ids]
    tile_grads = jnp.einsum(
        "tji,tjo->tio", adjacency, grad_rows, preferred_element_type=jnp.float32
    )
    slot_onehot = (tile_ids[:, None] == jnp.arange(slot_count)[None, :]).astype(jnp.float32)
    slot_grads = jnp.einsum("ts,tio->sio", slot_onehot, tile_grads, precision=highest).astype(
        jnp.bfloat16
    )
    slot_grads = slot_grads.reshape(shards, capacity, BLK, width_out)
    returned = lax.all_to_all(slot_grads, "shard", split_axis=0, concat_axis=0, tiled=True)
    owner_key = (owner_rel * nblocks + send_block).reshape(-1)
    owner_onehot = (owner_key[:, None] == jnp.arange(relations * nblocks)[None, :]).astype(
        jnp.bfloat16
    )
    source_grads = jnp.einsum(
        "sk,sio->kio",
        owner_onehot,
        returned.reshape(slot_count, BLK, width_out),
        preferred_element_type=jnp.float32,
    )
    source_grads = source_grads.astype(jnp.bfloat16).reshape(relations, nblocks * BLK, width_out)
    through_rel = jnp.einsum(
        "rno,rco->nc", source_grads, rel_weights, preferred_element_type=jnp.float32
    )
    feature_sum = lax.psum_scatter(
        through_rel + jnp.dot(d_out, root_weight.T, preferred_element_type=jnp.float32),
        "rep",
        scatter_dimension=0,
        tiled=True,
    )
    grad_feats = feature_sum.astype(jnp.bfloat16)
    relation_grads = jnp.einsum(
        "nc,rno->cro", feats, source_grads, preferred_element_type=jnp.float32
    )
    root_grad = jnp.dot(feats.T, d_out, preferred_element_type=jnp.float32)
    stacked = jnp.concatenate([relation_grads, root_grad[:, None, :]], axis=1)
    reduced = lax.psum_scatter(stacked, "shard", scatter_dimension=0, tiled=True)
    grad_bases = jnp.einsum(
        "rb,iro->bio", coef.astype(jnp.float32), reduced[:, :relations], precision=highest
    )
    grad_root = reduced[:, relations]
    row_count = reduced.shape[0]
    base_rows = lax.dynamic_slice_in_dim(bases, lax.axis_index("shard") * row_count, row_count, 1)
    partial_coef = jnp.einsum(
        "iro,bio->rb", reduced[:, :relations], base_rows.astype(jnp.float32), precision=highest
    )
    grad_coef = lax.psum(partial_coef, ("shard", "rep"))
    return (output, grad_feats, grad_bases, grad_root, grad_coef)


def solution(mesh):
    placed = (
        P("shard", None),
        P(None, None, "rep"),
        P(),
        P(None, "rep"),
        P("shard", None, None),
        P("shard", None, None),
        P("shard", None),
        P("shard", None),
        P("shard", None, None, None),
        P("shard", "rep"),
    )
    return jax.shard_map(
        body,
        mesh=mesh,
        in_specs=placed,
        out_specs=(
            P("shard", "rep"),
            P(("shard", "rep"), None),
            P(None, "shard", "rep"),
            P("shard", "rep"),
            P(),
        ),
        check_vma=False,
    )
```

profile of v0, /device:TPU:1, one launch (start us, length us, event | category | flops | bytes accessed | tf_op | source)
XLA Modules:
  0.0 624.1 jit_solution(11586295730918086103)
XLA Ops:
  7.2 1.5 copy.60
  8.7 9.6 %all-to-all-start.1 = ((s32[32,1,2]{2,1,0:T(1,128)}), s32[32,1,2]{2,1,0:T(1,128)S(1)}, u32[]{:S(2)}, u32[]{:S(2)}) async-start(s32[32,1,2]{2,1,0:T(1,128)} %copy.60), calls=%async_computation.1 | async-start | bytes 32768 | tf_op jit(solution)/shard_map/all_to_all | solution.py:34
  19.0 10.8 %gather_fusion.3 = bf16[256,128,256]{2,1,0:T(8,128)(2,1)} fusion(bf16[8,128,256]{2,1,0:T(8,128)(2,1)} %bitcast.87, s32[1024]{0:T(1024)S(1)} %pad_clamp_fusion), kind=kCustom, calls=%fused_computation.3 | custom fusion | bytes 33555456 | tf_op jit(solution)/shard_map/gather | solution.py:50
  29.8 20.1 %convolution_bitcast_fusion = f32[256,128,256]{1,2,0:T(8,128)} fusion(bf16[256,128,256]{2,1,0:T(8,128)(2,1)} %gather_fusion.3, bf16[1,256,128,128]{3,2,1,0:T(8,128)(2,1)} %param.18), kind=kOutput, calls=%fused_computation.5 | convolution fusion | flops 2147483648 | bytes 58720256 | tf_op jit(solution)/shard_map/tji,tjo->tio/dot_general | solution.py:51
  49.9 33.4 %copy.63 = f32[256,128,256]{2,0,1:T(8,128)} copy(f32[256,128,256]{1,2,0:T(8,128)} %convolution_bitcast_fusion) | data formatting | bytes 67108864 | tf_op jit(solution)/shard_map/tji,tjo->tio/dot_general | solution.py:51
  83.3 19.2 %convolution_convert_fusion.1 = bf16[64,128,256]{2,0,1:T(8,128)(2,1)} fusion(f32[256,128,256]{2,0,1:T(8,128)} %copy.63, s32[256]{0:T(256)S(1)} %bitcast.99), kind=kOutput, calls=%fused_computation.11 | convolution fusion | flops 6444564480 | bytes 37749760 | tf_op jit(solution)/shard_map/ts,tio->sio/dot_general | solution.py:55
  102.4 7.2 %reshape.172 = bf16[32,2,128,256]{3,1,0,2:T(2,128)(2,1)} reshape(bf16[64,128,256]{2,0,1:T(8,128)(2,1)} %convolution_convert_fusion.1) | data formatting | bytes 8388608 | tf_op jit(solution)/shard_map/reshape | solution.py:58
  109.7 8.5 %copy.64 = bf16[32,2,128,256]{3,1,2,0:T(2,128)(2,1)} copy(bf16[32,2,128,256]{3,1,0,2:T(2,128)(2,1)} %reshape.172) | data formatting | bytes 8388608 | tf_op jit(solution)/shard_map/reshape | solution.py:58
  118.2 7.6 %all-to-all-start.2 = ((bf16[32,2,128,256]{3,1,2,0:T(2,128)(2,1)}), bf16[32,2,128,256]{3,1,2,0:T(2,128)(2,1)}, u32[]{:S(2)}, u32[]{:S(2)}) async-start(bf16[32,2,128,256]{3,1,2,0:T(2,128)(2,1)} %copy.64), calls=%async_computation.2 | async-start | bytes 8388608 | tf_op jit(solution)/shard_map/all_to_all | solution.py:59
  125.8 11.4 %reduce-scatter.5.cloned.1.call-start = ((), (), s32[]{:S(2)}) async-start(), calls=%async_computation.6 | async-start | bytes 6488064 | tf_op jit(solution)/shard_map/reduce_scatter | solution.py:86
  138.2 39.7 %all-to-all-done.2 = bf16[32,2,128,256]{3,1,2,0:T(2,128)(2,1)} async-done(((bf16[32,2,128,256]{3,1,2,0:T(2,128)(2,1)}), bf16[32,2,128,256]{3,1,2,0:T(2,128)(2,1)}, u32[]{:S(2)}, u32[]{:S(2)}) %all-to-all-start.2) | async-done | bytes 4194336 | tf_op jit(solution)/shard_map/all_to_all | solution.py:59
  178.0 8.9 %copy.65 = bf16[32,2,128,256]{3,1,0,2:T(2,128)(2,1)} copy(bf16[32,2,128,256]{3,1,2,0:T(2,128)(2,1)} %all-to-all-done.2) | data formatting | bytes 8388608 | tf_op jit(solution)/shard_map/all_to_all | solution.py:59
  186.9 7.2 %reshape.173 = bf16[64,128,256]{2,0,1:T(8,128)(2,1)} reshape(bf16[32,2,128,256]{3,1,0,2:T(2,128)(2,1)} %copy.65) | data formatting | bytes 8388608 | tf_op jit(solution)/shard_map/reshape | solution.py:67
  194.1 3.0 convolution_convert_fusion.3
  197.7 2.3 convolution_bitcast_fusion.2
  200.0 2.6 pad_maximum_fusion
  202.6 6.3 %copy.69 = f32[768,6,256]{2,1,0:T(8,128)} copy(f32[768,6,256]{0,2,1:T(8,128)} %pad_maximum_fusion) | data formatting | bytes 9437184 | tf_op jit(solution)/shard_map/concatenate | solution.py:85
  209.1 7.2 %gather_fusion = bf16[64,128,768]{2,1,0:T(8,128)(2,1)} fusion(bf16[8,128,768]{2,1,0:T(8,128)(2,1)S(1)} %bitcast.86, s32[1024]{0:T(1024)S(1)} %pad_clamp_fusion.3), kind=kCustom, calls=%fused_computation | custom fusion | bytes 25166080 | tf_op jit(solution)/shard_map/gather | solution.py:40
  216.3 7.3 %all-to-all-start = ((bf16[32,2,128,768]{3,2,1,0:T(8,128)(2,1)}), bf16[32,2,128,768]{3,2,1,0:T(8,128)(2,1)}, u32[]{:S(2)}, u32[]{:S(2)}) async-start(bf16[32,2,128,768]{3,2,1,0:T(8,128)(2,1)} %bitcast.90), calls=%async_computation | async-start | bytes 25165824 | tf_op jit(solution)/shard_map/all_to_all | solution.py:41
  223.7 2.7 copy.78
  228.2 2.2 fusion.19
  230.5 2.3 bitcast_add_fusion
  235.0 11.0 %gather_fusion.1 = bf16[64,768,256]{2,1,0:T(8,128)(2,1)} fusion(bf16[5,768,256]{2,1,0:T(8,128)(2,1)S(1)} %bitcast.89, s32[1024]{0:T(1024)S(1)} %pad_clamp_fusion.2), kind=kCustom, calls=%fused_computation.1 | custom fusion | bytes 50331904 | tf_op jit(solution)/shard_map/gather | solution.py:39
  246.8 159.7 %reduce-scatter.5.cloned.1.call-done = f32[24,6,256]{2,1,0:T(8,128)} async-done(((f32[768,6,256]{2,1,0:T(8,128)}), f32[24,6,256]{2,1,0:T(8,128)}) %reduce-scatter.5.cloned.1.call-update) | async-done | bytes 147472 | tf_op jit(solution)/shard_map/reduce_scatter | solution.py:86
  407.7 40.2 %reduce-scatter.3.cloned.1.call-done = f32[256,768]{1,0:T(8,128)} async-done(((f32[1024,768]{1,0:T(8,128)}), f32[256,768]{1,0:T(8,128)}) %reduce-scatter.3.cloned.1.call-update) | async-done | bytes 786448 | tf_op jit(solution)/shard_map/reduce_scatter | solution.py:74
  447.9 1.9 convert_element_type.28
  449.9 64.9 %psum.7 = f32[5,4]{0,1:T(4,128)} all-reduce(f32[5,4]{0,1:T(4,128)S(1)} %convolution_bitcast_fusion.5), channel_id=1, replica_groups=mesh['shard'=32,'rep'=4] {'shard','rep'}, use_global_device_ids=true, to_apply=%region_2.0 | all-reduce | flops 20 | bytes 160 | tf_op jit(solution)/shard_map/psum | solution.py:96
  518.1 15.7 %convolution_convert_fusion.2 = bf16[64,128,256]{2,1,0:T(8,128)(2,1)} fusion(bf16[64,128,768]{2,1,0:T(8,128)(2,1)} %bitcast.5, bf16[64,768,256]{2,1,0:T(8,128)(2,1)} %gather_fusion.1), kind=kOutput, calls=%fused_computation.12 | convolution fusion | flops 3223322624 | bytes 41943040 | tf_op jit(solution)/shard_map/snc,sco->sno/dot_general | solution.py:11
  533.9 12.0 %gather_fusion.2 = bf16[256,128,256]{2,1,0:T(8,128)(2,1)} fusion(bf16[64,128,256]{2,1,0:T(8,128)(2,1)} %convolution_convert_fusion.2, s32[1024]{0:T(1024)S(1)} %pad_clamp_fusion.1), kind=kCustom, calls=%fused_computation.2 | custom fusion | bytes 33555456 | tf_op jit(solution)/shard_map/gather | solution.py:43
  545.9 20.1 %convolution_bitcast_fusion.1 = f32[256,128,256]{1,2,0:T(8,128)} fusion(bf16[256,128,256]{2,1,0:T(8,128)(2,1)} %gather_fusion.2, bf16[1,256,128,128]{3,2,1,0:T(8,128)(2,1)} %param.18), kind=kOutput, calls=%fused_computation.6 | convolution fusion | flops 2147483648 | bytes 58720256 | tf_op jit(solution)/shard_map/tij,tjo->tio/dot_general | solution.py:44
  566.0 33.4 %copy.58 = f32[256,128,256]{2,0,1:T(8,128)} copy(f32[256,128,256]{1,2,0:T(8,128)} %convolution_bitcast_fusion.1) | data formatting | bytes 67108864 | tf_op jit(solution)/shard_map/tij,tjo->tio/dot_general | solution.py:44
  599.4 15.8 %fusion.14 = f32[8,128,256]{2,0,1:T(8,128)S(1)} fusion(f32[256,128,256]{2,0,1:T(8,128)} %copy.58, s32[256]{0:T(256)S(1)} %bitcast.98), kind=kOutput, calls=%fused_computation.35 | convolution fusion | flops 805308416 | bytes 34604032 | tf_op jit(solution)/shard_map/tb,tio->bio/dot_general | solution.py:46
  (62 shorter events, 13.7 us)
Async XLA Ops:
  7.2 130.3 %copy-start = (bf16[1024,768]{1,0:T(8,128)(2,1)S(1)}, bf16[1024,768]{1,0:T(8,128)(2,1)}, u32[]{:S(2)}) copy-start(bf16[1024,768]{1,0:T(8,128)(2,1)} %param.10) | copy-start | bytes 4718596
  8.7 109.5 %all-to-all-start.1 = ((s32[32,1,2]{2,1,0:T(1,128)}), s32[32,1,2]{2,1,0:T(1,128)S(1)}, u32[]{:S(2)}, u32[]{:S(2)}) async-start(s32[32,1,2]{2,1,0:T(1,128)} %copy.60), calls=%async_computation.1 | async-start | bytes 32768 | tf_op jit(solution)/shard_map/all_to_all | solution.py:34
  49.9 33.4 %copy-start.9 = (s32[1,256]{1,0:T(1,128)S(1)}, s32[1,256]{1,0:T(1,128)}, u32[]{:S(2)}) copy-start(s32[1,256]{1,0:T(1,128)} %param.16) | copy-start | bytes 3076
  118.2 19.0 %copy-start.11 = (s32[1,32,2]{1,2,0:T(2,128)S(1)}, s32[1,32,2]{1,2,0:T(2,128)}, u32[]{:S(2)}) copy-start(s32[1,32,2]{1,2,0:T(2,128)} %param.14) | copy-start | bytes 772
  118.2 19.2 %copy-start.1 = (bf16[1024,256]{1,0:T(8,128)(2,1)S(1)}, bf16[1024,256]{1,0:T(8,128)(2,1)}, u32[]{:S(2)}) copy-start(bf16[1024,256]{1,0:T(8,128)(2,1)} %param.19) | copy-start | bytes 1572868
  118.2 59.8 %all-to-all-start.2 = ((bf16[32,2,128,256]{3,1,2,0:T(2,128)(2,1)}), bf16[32,2,128,256]{3,1,2,0:T(2,128)(2,1)}, u32[]{:S(2)}, u32[]{:S(2)}) async-start(bf16[32,2,128,256]{3,1,2,0:T(2,128)(2,1)} %copy.64), calls=%async_computation.2 | async-start | bytes 8388608 | tf_op jit(solution)/shard_map/all_to_all | solution.py:59
  125.8 280.7 %reduce-scatter.5.cloned.1.call-start = ((), (), s32[]{:S(2)}) async-start(), calls=%async_computation.6 | async-start | bytes 6488064 | tf_op jit(solution)/shard_map/reduce_scatter | solution.py:86
  197.7 2.3 copy-start.4
  216.3 10.0 %copy-start.12 = (bf16[5,4]{0,1:T(4,128)(2,1)S(1)}, bf16[5,4]{0,1:T(4,128)(2,1)}, u32[]{:S(2)}) copy-start(bf16[5,4]{0,1:T(4,128)(2,1)} %param.12) | copy-start | bytes 124
  216.3 301.8 %all-to-all-start = ((bf16[32,2,128,768]{3,2,1,0:T(8,128)(2,1)}), bf16[32,2,128,768]{3,2,1,0:T(8,128)(2,1)}, u32[]{:S(2)}, u32[]{:S(2)}) async-start(bf16[32,2,128,768]{3,2,1,0:T(8,128)(2,1)} %bitcast.90), calls=%async_computation | async-start | bytes 25165824 | tf_op jit(solution)/shard_map/all_to_all | solution.py:41
  223.6 224.3 %reduce-scatter.3.cloned.1.call-start = ((), (), s32[]{:S(2)}) async-start(), calls=%async_computation.5 | async-start | bytes 3932160 | tf_op jit(solution)/shard_map/reduce_scatter | solution.py:74
  226.4 1.8 copy-start.5
  228.2 2.3 copy-start.2
  228.2 2.2 copy-start.6
  232.8 2.2 copy-start.3
  235.0 11.0 %copy-start.10 = (s32[1,256]{1,0:T(1,128)S(1)}, s32[1,256]{1,0:T(1,128)}, u32[]{:S(2)}) copy-start(s32[1,256]{1,0:T(1,128)} %param.16) | copy-start | bytes 3076
  235.0 279.8 %copy-start.13 = (bf16[5,4]{0,1:T(4,128)(2,1)S(1)}, bf16[5,4]{0,1:T(4,128)(2,1)}, u32[]{:S(2)}) copy-start(bf16[5,4]{0,1:T(4,128)(2,1)} %param.12) | copy-start | bytes 124
  566.0 33.4 %copy-start.8 = (s32[1,256]{1,0:T(1,128)S(1)}, s32[1,256]{1,0:T(1,128)}, u32[]{:S(2)}) copy-start(s32[1,256]{1,0:T(1,128)} %param.17) | copy-start | bytes 3076
  599.4 16.1 %copy-start.7 = (bf16[768,256]{1,0:T(8,128)(2,1)S(1)}, bf16[768,256]{1,0:T(8,128)(2,1)}, u32[]{:S(2)}) copy-start(bf16[768,256]{1,0:T(8,128)(2,1)} %param.13) | copy-start | bytes 1179652
Sparse Core Ops, SparseCore 0:
  209.0 197.4 reduce-scatter.4
  409.0 38.8 reduce-scatter.2
where the time goes:
time: 635 us; the launch traced here: 624 us
  waiting for transfers between devices  240 us (38%)
  local copies, waits for them, and re-layouts  157 us (25%)
  matrix products  106 us (17%)
  blocking collectives  64.9 us (10%)
  starting transfers between devices  35.9 us (6%)
  between operations  14.7 us (2%)
    reduce_scatter x1, waiting for transfers between devices, body(): lax.psum_scatter(stacked, 'shard', scatter_dimension=0, tiled=True)  160 us
    psum x1, blocking collectives, body(): grad_coef = lax.psum(partial_coef, ('shard', 'rep'))  64.9 us
    reduce_scatter x1, waiting for transfers between devices, body(): lax.psum_scatter(through_rel + jnp.dot(d_out, root_weight.T, preferred_el...  40.2 us
    all_to_all x1, waiting for transfers between devices, body(): lax.all_to_all(slot_grads, 'shard', split_axis=0, concat_axis=0, tiled=True)  39.7 us
    dot_general x1, local copies, waits for them, and re-layouts, body(): jnp.einsum('tij,tjo->tio', adjacency, tile_msgs, preferred_element_type=j...  33.4 us
    dot_general x1, local copies, waits for them, and re-layouts, body(): jnp.einsum('tji,tjo->tio', adjacency, grad_rows, preferred_element_type=j...  33.4 us
    dot_general x1, matrix products, body(): jnp.einsum('tij,tjo->tio', adjacency, tile_msgs, preferred_element_type=j...  20.1 us
    dot_general x1, matrix products, body(): jnp.einsum('tji,tjo->tio', adjacency, grad_rows, preferred_element_type=j...  20.1 us
  transfers between devices with their start and end apart: 5, of which 3 were waited for; matrix products, arithmetic and copies ran while one was open for 22% of the time, Pallas kernels for 0%

commit v1 on v0

--- a/solution.py
+++ b/solution.py
@@ -93,7 +93,7 @@
     partial_coef = jnp.einsum(
         "iro,bio->rb", reduced[:, :relations], base_rows.astype(jnp.float32), precision=highest
     )
-    grad_coef = lax.psum(partial_coef, ("shard", "rep"))
+    grad_coef = jnp.sum(lax.all_gather(partial_coef, ("shard", "rep")), axis=0)
     return (output, grad_feats, grad_bases, grad_root, grad_coef)
 
 

time: 635 us -> 594 us (0.935)
  waiting for transfers between devices: 240 us -> 202 us
  starting transfers between devices: 35.9 us -> 24.8 us
    all_gather x0 -> x1, blocking collectives: none -> 69.4 us  [body(): grad_coef = jnp.sum(lax.all_gather(partial_coef, ('shard', 'rep')), axis=0)]
    psum x1 -> x0, blocking collectives: 64.9 us -> none  [body(): grad_coef = lax.psum(partial_coef, ('shard', 'rep'))]
    reduce_scatter x1, waiting for transfers between devices: 40.2 us -> 0.01 us  [body(): lax.psum_scatter(through_rel + jnp.dot(d_out, root_weight.T, preferred_el...]
    reduce_scatter x1, starting transfers between devices: 11.4 us -> 0.25 us  [body(): lax.psum_scatter(stacked, 'shard', scatter_dimension=0, tiled=True)]
    all_to_all x1, waiting for transfers between devices: 39.7 us -> 47.3 us  [body(): lax.all_to_all(slot_grads, 'shard', split_axis=0, concat_axis=0, tiled=True)]
  transfers between devices with their start and end apart: 5 -> 5, of which waited for: 3 -> 2; matrix products, arithmetic and copies ran while one was open for 22% -> 25% of each run, Pallas kernels for 0% -> 0%
where the time goes in v1:
time: 594 us; the launch traced here: 582 us
  waiting for transfers between devices  202 us (34%)
  local copies, waits for them, and re-layouts  156 us (26%)
  matrix products  108 us (18%)
  blocking collectives  69.4 us (12%)
  starting transfers between devices  24.8 us (4%)
  between operations  14.7 us (2%)
  other arithmetic  6.76 us (1%)
    reduce_scatter x1, waiting for transfers between devices, body(): lax.psum_scatter(stacked, 'shard', scatter_dimension=0, tiled=True)  155 us
    all_gather x1, blocking collectives, body(): grad_coef = jnp.sum(lax.all_gather(partial_coef, ('shard', 'rep')), axis=0)  69.4 us
    all_to_all x1, waiting for transfers between devices, body(): lax.all_to_all(slot_grads, 'shard', split_axis=0, concat_axis=0, tiled=True)  47.3 us
    dot_general x1, local copies, waits for them, and re-layouts, body(): jnp.einsum('tji,tjo->tio', adjacency, grad_rows, preferred_element_type=j...  33.4 us
    dot_general x1, local copies, waits for them, and re-layouts, body(): jnp.einsum('tij,tjo->tio', adjacency, tile_msgs, preferred_element_type=j...  33.4 us
    dot_general x1, matrix products, body(): jnp.einsum('tij,tjo->tio', adjacency, tile_msgs, preferred_element_type=j...  20.1 us
    dot_general x1, matrix products, body(): jnp.einsum('tji,tjo->tio', adjacency, grad_rows, preferred_element_type=j...  20.1 us
    dot_general x1, matrix products, body(): jnp.einsum('ts,tio->sio', slot_onehot, tile_grads, precision=highest)  19.2 us
  transfers between devices with their start and end apart: 5, of which 2 were waited for; matrix products, arithmetic and copies ran while one was open for 25% of the time, Pallas kernels for 0%

profile of v1, /device:TPU:1, one launch (start us, length us, event | category | flops | bytes accessed | tf_op | source)
XLA Modules:
  0.0 581.9 jit_solution(5979839053594988120)
XLA Ops:
  7.2 1.5 copy.60
  8.7 9.6 %all-to-all-start.1 = ((s32[32,1,2]{2,1,0:T(1,128)}), s32[32,1,2]{2,1,0:T(1,128)S(1)}, u32[]{:S(2)}, u32[]{:S(2)}) async-start(s32[32,1,2]{2,1,0:T(1,128)} %copy.60), calls=%async_computation.1 | async-start | bytes 32768 | tf_op jit(solution)/shard_map/all_to_all | solution.py:34
  19.0 10.8 %gather_fusion.3 = bf16[256,128,256]{2,1,0:T(8,128)(2,1)} fusion(bf16[8,128,256]{2,1,0:T(8,128)(2,1)} %bitcast.88, s32[1024]{0:T(1024)S(1)} %pad_clamp_fusion), kind=kCustom, calls=%fused_computation.3 | custom fusion | bytes 33555456 | tf_op jit(solution)/shard_map/gather | solution.py:50
  29.8 20.1 %convolution_bitcast_fusion = f32[256,128,256]{1,2,0:T(8,128)} fusion(bf16[256,128,256]{2,1,0:T(8,128)(2,1)} %gather_fusion.3, bf16[1,256,128,128]{3,2,1,0:T(8,128)(2,1)} %param.18), kind=kOutput, calls=%fused_computation.5 | convolution fusion | flops 2147483648 | bytes 58720256 | tf_op jit(solution)/shard_map/tji,tjo->tio/dot_general | solution.py:51
  49.9 33.4 %copy.63 = f32[256,128,256]{2,0,1:T(8,128)} copy(f32[256,128,256]{1,2,0:T(8,128)} %convolution_bitcast_fusion) | data formatting | bytes 67108864 | tf_op jit(solution)/shard_map/tji,tjo->tio/dot_general | solution.py:51
  83.3 19.2 %convolution_convert_fusion.1 = bf16[64,128,256]{2,0,1:T(8,128)(2,1)} fusion(f32[256,128,256]{2,0,1:T(8,128)} %copy.63, s32[256]{0:T(256)S(1)} %bitcast.100), kind=kOutput, calls=%fused_computation.11 | convolution fusion | flops 6444564480 | bytes 37749760 | tf_op jit(solution)/shard_map/ts,tio->sio/dot_general | solution.py:55
  102.4 7.2 %reshape.172 = bf16[32,2,128,256]{3,1,0,2:T(2,128)(2,1)} reshape(bf16[64,128,256]{2,0,1:T(8,128)(2,1)} %convolution_convert_fusion.1) | data formatting | bytes 8388608 | tf_op jit(solution)/shard_map/reshape | solution.py:58
  109.6 8.5 %copy.64 = bf16[32,2,128,256]{3,1,2,0:T(2,128)(2,1)} copy(bf16[32,2,128,256]{3,1,0,2:T(2,128)(2,1)} %reshape.172) | data formatting | bytes 8388608 | tf_op jit(solution)/shard_map/reshape | solution.py:58
  118.1 7.6 %all-to-all-start.2 = ((bf16[32,2,128,256]{3,1,2,0:T(2,128)(2,1)}), bf16[32,2,128,256]{3,1,2,0:T(2,128)(2,1)}, u32[]{:S(2)}, u32[]{:S(2)}) async-start(bf16[32,2,128,256]{3,1,2,0:T(2,128)(2,1)} %copy.64), calls=%async_computation.2 | async-start | bytes 8388608 | tf_op jit(solution)/shard_map/all_to_all | solution.py:59
  127.4 1.3 convolution_convert_fusion
  128.7 1.8 copy.84
  130.6 47.3 %all-to-all-done.2 = bf16[32,2,128,256]{3,1,2,0:T(2,128)(2,1)} async-done(((bf16[32,2,128,256]{3,1,2,0:T(2,128)(2,1)}), bf16[32,2,128,256]{3,1,2,0:T(2,128)(2,1)}, u32[]{:S(2)}, u32[]{:S(2)}) %all-to-all-start.2) | async-done | bytes 4194336 | tf_op jit(solution)/shard_map/all_to_all | solution.py:59
  177.9 8.9 %copy.65 = bf16[32,2,128,256]{3,1,0,2:T(2,128)(2,1)} copy(bf16[32,2,128,256]{3,1,2,0:T(2,128)(2,1)} %all-to-all-done.2) | data formatting | bytes 8388608 | tf_op jit(solution)/shard_map/all_to_all | solution.py:59
  186.8 7.2 %reshape.173 = bf16[64,128,256]{2,0,1:T(8,128)(2,1)} reshape(bf16[32,2,128,256]{3,1,0,2:T(2,128)(2,1)} %copy.65) | data formatting | bytes 8388608 | tf_op jit(solution)/shard_map/reshape | solution.py:67
  194.0 3.2 convolution_convert_fusion.3
  197.8 2.2 fusion.19
  200.1 2.3 bitcast_add_fusion
  202.7 7.2 %gather_fusion = bf16[64,128,768]{2,1,0:T(8,128)(2,1)} fusion(bf16[8,128,768]{2,1,0:T(8,128)(2,1)S(1)} %bitcast.87, s32[1024]{0:T(1024)S(1)} %pad_clamp_fusion.3), kind=kCustom, calls=%fused_computation | custom fusion | bytes 25166080 | tf_op jit(solution)/shard_map/gather | solution.py:40
  209.9 7.1 %all-to-all-start = ((bf16[32,2,128,768]{3,2,1,0:T(8,128)(2,1)}), bf16[32,2,128,768]{3,2,1,0:T(8,128)(2,1)}, u32[]{:S(2)}, u32[]{:S(2)}) async-start(bf16[32,2,128,768]{3,2,1,0:T(8,128)(2,1)} %bitcast.91), calls=%async_computation | async-start | bytes 25165824 | tf_op jit(solution)/shard_map/all_to_all | solution.py:41
  217.9 4.0 convolution_bitcast_fusion.2
  222.0 2.7 pad_maximum_fusion
  224.7 6.3 %copy.69 = f32[768,6,256]{2,1,0:T(8,128)} copy(f32[768,6,256]{0,2,1:T(8,128)} %pad_maximum_fusion) | data formatting | bytes 9437184 | tf_op jit(solution)/shard_map/concatenate | solution.py:85
  233.2 10.5 %gather_fusion.1 = bf16[64,768,256]{2,1,0:T(8,128)(2,1)} fusion(bf16[5,768,256]{2,1,0:T(8,128)(2,1)S(1)} %bitcast.90, s32[1024]{0:T(1024)S(1)} %pad_clamp_fusion.2), kind=kCustom, calls=%fused_computation.1 | custom fusion | bytes 50331904 | tf_op jit(solution)/shard_map/gather | solution.py:39
  244.6 1.9 convert_element_type.28
  246.5 154.7 %reduce-scatter.5.cloned.1.call-done = f32[24,6,256]{2,1,0:T(8,128)} async-done(((f32[768,6,256]{2,1,0:T(8,128)}), f32[24,6,256]{2,1,0:T(8,128)}) %reduce-scatter.5.cloned.1.call-update) | async-done | bytes 147472 | tf_op jit(solution)/shard_map/reduce_scatter | solution.py:86
  405.8 69.4 %all-gather.1 = f32[128,5,4]{1,2,0:T(4,128)S(1)} all-gather(f32[1,5,4]{1,2,0:T(4,128)S(1)} %convolution_bitcast_fusion.5), channel_id=2, replica_groups=mesh['shard'=32,'rep'=4] {'shard','rep'}, dimensions={0}, use_global_device_ids=true | all-gather | bytes 10320 | tf_op jit(solution)/shard_map/all_gather | solution.py:96
  476.0 15.7 %convolution_convert_fusion.2 = bf16[64,128,256]{2,1,0:T(8,128)(2,1)} fusion(bf16[64,128,768]{2,1,0:T(8,128)(2,1)} %bitcast.5, bf16[64,768,256]{2,1,0:T(8,128)(2,1)} %gather_fusion.1), kind=kOutput, calls=%fused_computation.12 | convolution fusion | flops 3223322624 | bytes 41943040 | tf_op jit(solution)/shard_map/snc,sco->sno/dot_general | solution.py:11
  491.7 12.0 %gather_fusion.2 = bf16[256,128,256]{2,1,0:T(8,128)(2,1)} fusion(bf16[64,128,256]{2,1,0:T(8,128)(2,1)} %convolution_convert_fusion.2, s32[1024]{0:T(1024)S(1)} %pad_clamp_fusion.1), kind=kCustom, calls=%fused_computation.2 | custom fusion | bytes 33555456 | tf_op jit(solution)/shard_map/gather | solution.py:43
  503.7 20.1 %convolution_bitcast_fusion.1 = f32[256,128,256]{1,2,0:T(8,128)} fusion(bf16[256,128,256]{2,1,0:T(8,128)(2,1)} %gather_fusion.2, bf16[1,256,128,128]{3,2,1,0:T(8,128)(2,1)} %param.18), kind=kOutput, calls=%fused_computation.6 | convolution fusion | flops 2147483648 | bytes 58720256 | tf_op jit(solution)/shard_map/tij,tjo->tio/dot_general | solution.py:44
  523.8 33.4 %copy.58 = f32[256,128,256]{2,0,1:T(8,128)} copy(f32[256,128,256]{1,2,0:T(8,128)} %convolution_bitcast_fusion.1) | data formatting | bytes 67108864 | tf_op jit(solution)/shard_map/tij,tjo->tio/dot_general | solution.py:44
  557.2 15.8 %fusion.14 = f32[8,128,256]{2,0,1:T(8,128)S(1)} fusion(f32[256,128,256]{2,0,1:T(8,128)} %copy.58, s32[256]{0:T(256)S(1)} %bitcast.99), kind=kOutput, calls=%fused_computation.35 | convolution fusion | flops 805308416 | bytes 34604032 | tf_op jit(solution)/shard_map/tb,tio->bio/dot_general | solution.py:46
  573.3 1.4 fusion.3
  (63 shorter events, 12.9 us)
Async XLA Ops:
  7.2 195.5 %copy-start = (bf16[1024,768]{1,0:T(8,128)(2,1)S(1)}, bf16[1024,768]{1,0:T(8,128)(2,1)}, u32[]{:S(2)}) copy-start(bf16[1024,768]{1,0:T(8,128)(2,1)} %param.10) | copy-start | bytes 4718596
  8.7 109.5 %all-to-all-start.1 = ((s32[32,1,2]{2,1,0:T(1,128)}), s32[32,1,2]{2,1,0:T(1,128)S(1)}, u32[]{:S(2)}, u32[]{:S(2)}) async-start(s32[32,1,2]{2,1,0:T(1,128)} %copy.60), calls=%async_computation.1 | async-start | bytes 32768 | tf_op jit(solution)/shard_map/all_to_all | solution.py:34
  49.9 33.4 %copy-start.9 = (s32[1,256]{1,0:T(1,128)S(1)}, s32[1,256]{1,0:T(1,128)}, u32[]{:S(2)}) copy-start(s32[1,256]{1,0:T(1,128)} %param.16) | copy-start | bytes 3076
  118.1 7.8 %copy-start.11 = (s32[1,32,2]{1,2,0:T(2,128)S(1)}, s32[1,32,2]{1,2,0:T(2,128)}, u32[]{:S(2)}) copy-start(s32[1,32,2]{1,2,0:T(2,128)} %param.14) | copy-start | bytes 772
  118.1 8.0 %copy-start.5 = (bf16[4,768,256]{2,1,0:T(8,128)(2,1)S(1)}, bf16[4,768,256]{2,1,0:T(8,128)(2,1)}, u32[]{:S(2)}) copy-start(bf16[4,768,256]{2,1,0:T(8,128)(2,1)} %param.11) | copy-start | bytes 4718596
  118.1 9.2 %copy-start.12 = (bf16[5,4]{0,1:T(4,128)(2,1)S(1)}, bf16[5,4]{0,1:T(4,128)(2,1)}, u32[]{:S(2)}) copy-start(bf16[5,4]{0,1:T(4,128)(2,1)} %param.12) | copy-start | bytes 124
  118.1 59.8 %all-to-all-start.2 = ((bf16[32,2,128,256]{3,1,2,0:T(2,128)(2,1)}), bf16[32,2,128,256]{3,1,2,0:T(2,128)(2,1)}, u32[]{:S(2)}, u32[]{:S(2)}) async-start(bf16[32,2,128,256]{3,1,2,0:T(2,128)(2,1)} %copy.64), calls=%async_computation.2 | async-start | bytes 8388608 | tf_op jit(solution)/shard_map/all_to_all | solution.py:59
  125.7 118.8 %reduce-scatter.3.cloned.1.call-start = ((), (), s32[]{:S(2)}) async-start(), calls=%async_computation.5 | async-start | bytes 3932160 | tf_op jit(solution)/shard_map/reduce_scatter | solution.py:74
  194.0 3.8 copy-start.2
  197.8 2.3 copy-start.4
  197.8 2.3 copy-start.1
  197.8 2.3 copy-start.6
  209.9 266.0 %all-to-all-start = ((bf16[32,2,128,768]{3,2,1,0:T(8,128)(2,1)}), bf16[32,2,128,768]{3,2,1,0:T(8,128)(2,1)}, u32[]{:S(2)}, u32[]{:S(2)}) async-start(bf16[32,2,128,768]{3,2,1,0:T(8,128)(2,1)} %bitcast.91), calls=%async_computation | async-start | bytes 25165824 | tf_op jit(solution)/shard_map/all_to_all | solution.py:41
  217.1 184.1 %reduce-scatter.5.cloned.1.call-start = ((), (), s32[]{:S(2)}) async-start(), calls=%async_computation.6 | async-start | bytes 6488064 | tf_op jit(solution)/shard_map/reduce_scatter | solution.py:86
  231.0 2.2 copy-start.3
  233.2 10.5 %copy-start.10 = (s32[1,256]{1,0:T(1,128)S(1)}, s32[1,256]{1,0:T(1,128)}, u32[]{:S(2)}) copy-start(s32[1,256]{1,0:T(1,128)} %param.16) | copy-start | bytes 3076
  233.2 168.0 %copy-start.13 = (bf16[5,4]{0,1:T(4,128)(2,1)S(1)}, bf16[5,4]{0,1:T(4,128)(2,1)}, u32[]{:S(2)}) copy-start(bf16[5,4]{0,1:T(4,128)(2,1)} %param.12) | copy-start | bytes 124
  523.8 33.4 %copy-start.8 = (s32[1,256]{1,0:T(1,128)S(1)}, s32[1,256]{1,0:T(1,128)}, u32[]{:S(2)}) copy-start(s32[1,256]{1,0:T(1,128)} %param.17) | copy-start | bytes 3076
  557.2 16.1 %copy-start.7 = (bf16[768,256]{1,0:T(8,128)(2,1)S(1)}, bf16[768,256]{1,0:T(8,128)(2,1)}, u32[]{:S(2)}) copy-start(bf16[768,256]{1,0:T(8,128)(2,1)} %param.13) | copy-start | bytes 1179652
Sparse Core Ops, SparseCore 0:
  202.6 38.9 reduce-scatter.2
  245.4 155.7 reduce-scatter.4
